TPU v7x, 512 devices: a whole 4x8x8 slice. The times are simulated.
512 devices in a mesh: row: 32 (over z_lo, y), col: 16 (over x, z_hi, core).
Axes of the slice: x: 4, y: 8, z: 8 (z_hi: 2, z_lo: 4; z = z_hi * 4 + z_lo), core: 2. Of those that a mesh axis runs over, the one named last changes fastest.
Arguments:
- queries: bfloat16 [1, 32, 32, 64, 2048], P(None, 'row', 'col'), may hold values from -17 to 17
- keys: bfloat16 [1, 32, 32, 64, 2048], P(None, 'row', 'col'), may hold values from -5.5 to 5.5
- values: bfloat16 [1, 32, 32, 64, 2048], P(None, 'row', 'col'), may hold values from -6 to 6
- pool_keys: bfloat16 [1024, 16, 2048], P(('row', 'col')), may hold values from -6 to 6
- pool_values: bfloat16 [1024, 16, 2048], P(('row', 'col')), may hold values from -6 to 6
- top_keys: bfloat16 [1, 128, 2048], P(None, 'col'), may hold values from -6 to 6
- top_values: bfloat16 [1, 128, 2048], P(None, 'col'), may hold values from -6 to 6
- coarse_ids: int32 [1, 32, 32, 8], P(None, 'row', 'col'), may hold values from 0 to 1023, as said below
Outputs:
- attended: bfloat16 [1, 32, 32, 64, 2048], P(None, 'row', 'col')
Inputs may be any that keep to these rules, and one draw needn't show every extreme that they name: Entry coarse_ids[n, i, j, c] names a pool block held by the device that holds fine block (i, j) or by one of its eight neighbours in the mesh (no wrap); the device with row index r and col index q holds pool blocks (r * 16 + q) * 2 to (r * 16 + q + 1) * 2 - 1. The 8 entries of a fine block differ.
All inputs are finite; a program needn't handle non-finite values.
Results may differ from a plain program's by a relative error of at most 0.0049.
Values may be sent and summed in bfloat16 or wider, within the bound.
No kernel may reach another device: no remote copies, remote signals or barrier semaphores. Data moves between devices by JAX's collectives and lax.ppermute only.
A program may use at most 64 MiB of HBM per device.

v0:
```python
import math
import jax
import jax.numpy as jnp
from jax import lax
from jax.sharding import PartitionSpec as P

HEADS = 16
NEG_FILL = -1e30


def extended(block, sides, width):
    for axis, dim in sides:
        count = lax.axis_size(axis)
        forward = [(i, i + 1) for i in range(count - 1)]
        backward = [(target, source) for source, target in forward]
        low = lax.ppermute(
            lax.slice_in_dim(block, block.shape[dim] - width, None, axis=dim), axis, forward
        )
        high = lax.ppermute(lax.slice_in_dim(block, 0, width, axis=dim), axis, backward)
        block = jnp.concatenate([low, block, high], axis=dim)
    return block


def body(queries, keys, values, pool_keys, pool_values, top_keys, top_values, coarse_ids):
    images, brow_count, bcol_count, block_tokens, model_width = queries.shape
    head_count = HEADS
    head_width = model_width // head_count
    score_scale = 1.0 / math.sqrt(head_width)
    pool_blocks = pool_keys.shape[0]
    pool_tokens = pool_keys.shape[1]
    row_count = lax.axis_size("row")
    col_count = lax.axis_size("col")
    row_index = lax.axis_index("row")
    col_index = lax.axis_index("col")
    pool_key_grid = pool_keys.reshape(1, 1, 1, pool_blocks * pool_tokens, model_width)
    pool_value_grid = pool_values.reshape(1, 1, 1, pool_blocks * pool_tokens, model_width)
    near_keys, near_values = (
        extended(keys, (("row", 1), ("col", 2)), 1),
        extended(values, (("row", 1), ("col", 2)), 1),
    )
    around_keys, around_values = (
        extended(pool_key_grid, (("row", 1), ("col", 2)), 1),
        extended(pool_value_grid, (("row", 1), ("col", 2)), 1),
    )
    around_keys = around_keys.reshape(9 * pool_blocks, pool_tokens, model_width)
    around_values = around_values.reshape(9 * pool_blocks, pool_tokens, model_width)
    top_all_keys, top_all_values = (
        lax.all_gather(top_keys, "col", axis=1, tiled=True),
        lax.all_gather(top_values, "col", axis=1, tiled=True),
    )
    owner_device = coarse_ids // pool_blocks
    owner_row = owner_device // col_count
    owner_col = owner_device % col_count
    local_slot = (
        (owner_row - row_index + 1) * 3 + (owner_col - col_index + 1)
    ) * pool_blocks + coarse_ids % pool_blocks
    global_row = row_index * brow_count + jnp.arange(brow_count, dtype=jnp.int32)
    global_col = col_index * bcol_count + jnp.arange(bcol_count, dtype=jnp.int32)
    total_rows = brow_count * row_count
    total_cols = bcol_count * col_count
    blocks = brow_count * bcol_count
    coarse_length = coarse_ids.shape[-1] * pool_tokens
    valid_parts = []
    for row_step in range(3):
        row_valid = (global_row + row_step - 1 >= 0) & (global_row + row_step - 1 < total_rows)
        for col_step in range(3):
            col_valid = (global_col + col_step - 1 >= 0) & (global_col + col_step - 1 < total_cols)
            part_valid = (row_valid[:, None] & col_valid[None, :]).reshape(blocks, 1)
            valid_parts.append(jnp.broadcast_to(part_valid, (blocks, block_tokens)))
    valid_parts.append(jnp.ones((blocks, coarse_length), dtype=bool))
    list_valid = jnp.concatenate(valid_parts, axis=1).reshape(blocks, 1, 1, -1)

    def attend_image(image_items):
        query_image, key_image, value_image, slot_image, top_key_image, top_value_image = (
            image_items
        )
        query_heads = query_image.reshape(blocks, block_tokens, head_count, head_width)
        key_lists = []
        value_lists = []
        for row_step in range(3):
            for col_step in range(3):
                key_lists.append(
                    key_image[
                        row_step : row_step + brow_count, col_step : col_step + bcol_count
                    ].reshape(blocks, block_tokens, model_width)
                )
                value_lists.append(
                    value_image[
                        row_step : row_step + brow_count, col_step : col_step + bcol_count
                    ].reshape(blocks, block_tokens, model_width)
                )
        key_lists.append(around_keys[slot_image].reshape(blocks, coarse_length, model_width))
        value_lists.append(around_values[slot_image].reshape(blocks, coarse_length, model_width))
        key_list = jnp.concatenate(key_lists, axis=1).reshape(blocks, -1, head_count, head_width)
        value_list = jnp.concatenate(value_lists, axis=1).reshape(
            blocks, -1, head_count, head_width
        )
        near_scores = (
            jnp.einsum("bqhd,bkhd->bhqk", query_heads, key_list, preferred_element_type=jnp.float32)
            * score_scale
        )
        near_scores = jnp.where(list_valid, near_scores, NEG_FILL)
        top_key_heads = top_key_image.reshape(-1, head_count, head_width)
        top_value_heads = top_value_image.reshape(-1, head_count, head_width)
        top_scores = (
            jnp.einsum(
                "bqhd,khd->bhqk", query_heads, top_key_heads, preferred_element_type=jnp.float32
            )
            * score_scale
        )
        row_peak = jnp.maximum(
            jnp.max(near_scores, axis=-1, keepdims=True),
            jnp.max(top_scores, axis=-1, keepdims=True),
        )
        near_exponent = jnp.exp(near_scores - row_peak)
        top_exponent = jnp.exp(top_scores - row_peak)
        row_total = jnp.sum(near_exponent, axis=-1, keepdims=True) + jnp.sum(
            top_exponent, axis=-1, keepdims=True
        )
        near_weights = (near_exponent / row_total).astype(jnp.bfloat16)
        top_weights = (top_exponent / row_total).astype(jnp.bfloat16)
        result = jnp.einsum(
            "bhqk,bkhd->bqhd", near_weights, value_list, preferred_element_type=jnp.float32
        )
        result = result + jnp.einsum(
            "bhqk,khd->bqhd", top_weights, top_value_heads, preferred_element_type=jnp.float32
        )
        return result.reshape(brow_count, bcol_count, block_tokens, model_width).astype(
            jnp.bfloat16
        )

    return lax.map(
        attend_image, (queries, near_keys, near_values, local_slot, top_all_keys, top_all_values)
    )


def solution(mesh):
    placed = (
        P(None, "row", "col", None, None),
        P(None, "row", "col", None, None),
        P(None, "row", "col", None, None),
        P(("row", "col"), None, None),
        P(("row", "col"), None, None),
        P(None, "col", None),
        P(None, "col", None),
        P(None, "row", "col", None),
    )
    return jax.shard_map(
        body,
        mesh=mesh,
        in_specs=placed,
        out_specs=P(None, "row", "col", None, None),
        check_vma=False,
    )
```

profile of v0, /device:TPU:6, one launch (start us, length us, event | category | flops | bytes accessed | tf_op | source)
XLA Modules:
  0.0 241.0 jit_solution(14862765426312695609)
XLA Ops:
  0.0 3.6 %collective-permute-start = (bf16[1,1,2,64,2048]{4,3,2,1,0:T(8,128)(2,1)}, bf16[1,1,2,64,2048]{4,3,2,1,0:T(8,128)(2,1)S(1)}, u32[]{:S(2)}, u32[]{:S(2)}) collective-permute-start(bf16[1,1,2,64,2048]{4,3,2,1,0:T(8,128)(2,1)} %param.10), channel_id=1, source_target_pairs={{0,16},{16,32},{32,48},{48,64},{64,80},{80,96},{96,112},{112,128},... | collective-permute-start | bytes 1572872 | tf_op jit(solution)/shard_map/ppermute | solution.py:16
  3.6 1.3 collective-permute-start.1
  4.9 1.3 collective-permute-start.5
  6.2 5.8 %collective-permute-start.4 = (bf16[1,1,1,32,2048]{4,3,2,1,0:T(8,128)(2,1)}, bf16[1,1,1,32,2048]{4,3,2,1,0:T(8,128)(2,1)}, u32[]{:S(2)}, u32[]{:S(2)}) collective-permute-start(bf16[1,1,1,32,2048]{4,3,2,1,0:T(8,128)(2,1)} %bitcast.215), channel_id=1, source_target_pairs={{0,16},{16,32},{32,48},{48,64},{64,80},{80,96},{96,112},{112,128},... | collective-permute-start | bytes 393224 | tf_op jit(solution)/shard_map/ppermute | solution.py:16
  12.1 1.3 collective-permute-start.13
  13.4 0.5 broadcast_and_fusion.4
  13.9 0.6 broadcast_and_fusion.2
  14.5 0.6 broadcast_and_fusion
  15.1 0.7 compare_select_fusion
  15.9 0.6 pad_clamp_fusion
  16.5 1.1 copy.119
  17.8 35.2 %all_gather.6 = bf16[1,128,2048]{2,1,0:T(8,128)(2,1)S(1)} all-gather(bf16[1,8,2048]{2,1,0:T(8,128)(2,1)} %param.13), channel_id=1, replica_groups=mesh['row'=32,'col'=16] {'col'}, dimensions={1}, use_global_device_ids=true | all-gather | bytes 557056 | tf_op jit(solution)/shard_map/all_gather | solution.py:48
  53.6 0.4 bitcast_reduce_fusion.1
  54.0 27.7 %all_gather.7 = bf16[1,128,2048]{2,1,0:T(8,128)(2,1)S(1)} all-gather(bf16[1,8,2048]{2,1,0:T(8,128)(2,1)} %param.14), channel_id=1, replica_groups=mesh['row'=32,'col'=16] {'col'}, dimensions={1}, use_global_device_ids=true | all-gather | bytes 557056 | tf_op jit(solution)/shard_map/all_gather | solution.py:49
  81.8 1.0 copy.102
  83.0 0.7 broadcast_in_dim.42
  83.7 0.7 broadcast_in_dim.43
  84.4 0.7 broadcast_in_dim.44
  85.1 0.8 broadcast_in_dim.45
  85.9 0.7 broadcast_in_dim.46
  86.6 0.7 broadcast_in_dim.47
  87.4 0.7 concatenate.92
  88.1 8.0 %collective-permute-start.12 = (bf16[1,1,1,32,2048]{4,3,2,1,0:T(8,128)(2,1)S(1)}, bf16[1,1,1,32,2048]{4,3,2,1,0:T(8,128)(2,1)S(1)}, u32[]{:S(2)}, u32[]{:S(2)}) collective-permute-start(bf16[1,1,1,32,2048]{4,3,2,1,0:T(8,128)(2,1)S(1)} %bitcast.219), channel_id=1, source_target_pairs={{0,16},{16,32},{32,48},{48,64},{64,80},{80,96},{96,112},{112,128},... | collective-permute-start | bytes 393224 | tf_op jit(solution)/shard_map/ppermute | solution.py:16
  96.1 3.7 %collective-permute-start.8 = (bf16[1,1,2,64,2048]{4,3,2,1,0:T(8,128)(2,1)}, bf16[1,1,2,64,2048]{4,3,2,1,0:T(8,128)(2,1)S(1)}, u32[]{:S(2)}, u32[]{:S(2)}) collective-permute-start(bf16[1,1,2,64,2048]{4,3,2,1,0:T(8,128)(2,1)} %param.9), channel_id=1, source_target_pairs={{0,16},{16,32},{32,48},{48,64},{64,80},{80,96},{96,112},{112,128},... | collective-permute-start | bytes 1572872 | tf_op jit(solution)/shard_map/ppermute | solution.py:16
  99.7 1.0 pad_maximum_fusion.3
  100.8 1.3 collective-permute-start.9
  102.1 8.1 %collective-permute-start.7 = (bf16[1,3,1,32,2048]{4,3,2,1,0:T(8,128)(2,1)S(1)}, bf16[1,3,1,32,2048]{4,3,2,1,0:T(8,128)(2,1)S(1)}, u32[]{:S(2)}, u32[]{:S(2)}) collective-permute-start(bf16[1,3,1,32,2048]{4,3,2,1,0:T(8,128)(2,1)S(1)} %pad_maximum_fusion.3), channel_id=1, source_target_pairs={{1,0},{2,1},{3,2},{4,3},{5,4},{6,5},{7,6},{8,7},{9,8},{10,9},{11,1... | collective-permute-start | bytes 1179656 | tf_op jit(solution)/shard_map/ppermute | solution.py:19
  110.2 0.8 pad_maximum_fusion.2
  111.0 0.8 copy-done.2
  111.7 1.9 collective-permute-start.6
  113.7 1.1 constant_dynamic-update-slice_fusion.5
  114.7 1.1 constant_dynamic-update-slice_fusion.4
  115.8 8.4 %collective-permute-start.15 = (bf16[1,3,1,32,2048]{4,3,2,1,0:T(8,128)(2,1)}, bf16[1,3,1,32,2048]{4,3,2,1,0:T(8,128)(2,1)}, u32[]{:S(2)}, u32[]{:S(2)}) collective-permute-start(bf16[1,3,1,32,2048]{4,3,2,1,0:T(8,128)(2,1)} %pad_maximum_fusion.2), channel_id=1, source_target_pairs={{1,0},{2,1},{3,2},{4,3},{5,4},{6,5},{7,6},{8,7},{9,8},{10,9},{11,1... | collective-permute-start | bytes 1179656 | tf_op jit(solution)/shard_map/ppermute | solution.py:19
  124.3 1.1 constant_dynamic-update-slice_fusion.3
  125.4 1.3 fusion.19
  126.7 1.9 collective-permute-start.14
  128.6 0.8 constant_dynamic-update-slice_fusion.2
  129.4 1.9 constant_dynamic-update-slice_fusion.1
  131.3 8.4 %collective-permute-start.3 = (bf16[1,3,1,64,2048]{4,3,2,1,0:T(8,128)(2,1)}, bf16[1,3,1,64,2048]{4,3,2,1,0:T(8,128)(2,1)}, u32[]{:S(2)}, u32[]{:S(2)}) collective-permute-start(bf16[1,3,1,64,2048]{4,3,2,1,0:T(8,128)(2,1)} %get-tuple-element.59), channel_id=1, source_target_pairs={{1,0},{2,1},{3,2},{4,3},{5,4},{6,5},{7,6},{8,7},{9,8},{10,9},{11,1... | collective-permute-start | bytes 2359304 | tf_op jit(solution)/shard_map/ppermute | solution.py:19
  139.8 1.9 collective-permute-start.2
  141.7 2.1 pad_maximum_fusion.1
  143.8 0.9 constant_dynamic-update-slice_fusion
  144.7 3.0 %gather_fusion = bf16[16,16,2048]{2,1,0:T(8,128)(2,1)} fusion(bf16[18,16,2048]{2,1,0:T(8,128)(2,1)} %bitcast.168, s32[1024]{0:T(1024)} %pad_clamp_fusion), kind=kCustom, calls=%fused_computation | custom fusion | bytes 2097216 | tf_op jit(solution)/shard_map/while/body/eval_jaxpr/gather | solution.py:93
  147.7 2.4 %copy.129 = bf16[32,8,16,128]{3,2,1,0:T(8,128)(2,1)} copy(bf16[32,8,16,128]{3,1,2,0:T(8,128)(2,1)} %bitcast.173) | data formatting | bytes 2097152
  150.1 2.7 %fusion.18 = (bf16[1,3,1,64,2048]{4,3,2,1,0:T(8,128)(2,1)}, bf16[1,3,1,64,2048]{4,3,2,1,0:T(8,128)(2,1)}) fusion(bf16[1,3,2,64,2048]{4,3,2,1,0:T(8,128)(2,1)} %constant_dynamic-update-slice_fusion), kind=kLoop, calls=%fused_computation.87 | loop fusion | bytes 3145728 | tf_op jit(solution)/shard_map/slice | solution.py:17
  152.8 8.4 %collective-permute-start.11 = (bf16[1,3,1,64,2048]{4,3,2,1,0:T(8,128)(2,1)}, bf16[1,3,1,64,2048]{4,3,2,1,0:T(8,128)(2,1)}, u32[]{:S(2)}, u32[]{:S(2)}) collective-permute-start(bf16[1,3,1,64,2048]{4,3,2,1,0:T(8,128)(2,1)} %get-tuple-element.57), channel_id=1, source_target_pairs={{1,0},{2,1},{3,2},{4,3},{5,4},{6,5},{7,6},{8,7},{9,8},{10,9},{11,1... | collective-permute-start | bytes 2359304 | tf_op jit(solution)/shard_map/ppermute | solution.py:19
  161.3 1.9 collective-permute-start.10
  163.2 2.3 pad_maximum_fusion
  165.6 3.0 %gather_fusion.1 = bf16[16,16,2048]{2,1,0:T(8,128)(2,1)} fusion(bf16[18,16,2048]{2,1,0:T(8,128)(2,1)} %bitcast.169, s32[1024]{0:T(1024)} %pad_clamp_fusion), kind=kCustom, calls=%fused_computation.1 | custom fusion | bytes 2097216 | tf_op jit(solution)/shard_map/while/body/eval_jaxpr/gather | solution.py:92
  168.5 1.5 copy.118
  170.0 39.1 %collective-permute-done.2 = bf16[1,3,1,64,2048]{4,3,2,1,0:T(8,128)(2,1)} collective-permute-done((bf16[1,3,1,64,2048]{4,3,2,1,0:T(8,128)(2,1)}, bf16[1,3,1,64,2048]{4,3,2,1,0:T(8,128)(2,1)}, u32[]{:S(2)}, u32[]{:S(2)}) %collective-permute-start.2) | collective-permute-done | bytes 786464 | tf_op jit(solution)/shard_map/ppermute | solution.py:16
  209.1 1.7 maximum_bitcast_fusion.1
  210.9 0.8 fusion.17
  212.9 10.7 %collective-permute-done.10 = bf16[1,3,1,64,2048]{4,3,2,1,0:T(8,128)(2,1)} collective-permute-done((bf16[1,3,1,64,2048]{4,3,2,1,0:T(8,128)(2,1)}, bf16[1,3,1,64,2048]{4,3,2,1,0:T(8,128)(2,1)}, u32[]{:S(2)}, u32[]{:S(2)}) %collective-permute-start.10) | collective-permute-done | bytes 786464 | tf_op jit(solution)/shard_map/ppermute | solution.py:16
  223.6 2.2 maximum_bitcast_fusion
  225.8 0.8 fusion.16
  229.3 0.3 copy_dynamic-update-slice_fusion
  229.6 2.3 bitcast_reduce_fusion
  232.0 1.9 fusion.1
  233.9 0.7 fusion.8
  236.4 2.2 fusion.4
  238.6 1.0 fusion.6
  239.6 0.3 copy.105
  240.0 1.0 convert_element_type.27
  (78 shorter events, 6.5 us)
Async XLA Ops:
  0.0 99.7 %copy-start.3 = (bf16[2,16,2048]{2,1,0:T(8,128)(2,1)S(1)}, bf16[2,16,2048]{2,1,0:T(8,128)(2,1)}, u32[]{:S(2)}) copy-start(bf16[2,16,2048]{2,1,0:T(8,128)(2,1)} %param.12) | copy-start | bytes 393220
  0.0 88.1 %copy-start.4 = (bf16[2,16,2048]{2,1,0:T(8,128)(2,1)S(1)}, bf16[2,16,2048]{2,1,0:T(8,128)(2,1)}, u32[]{:S(2)}) copy-start(bf16[2,16,2048]{2,1,0:T(8,128)(2,1)} %param.11) | copy-start | bytes 393220
  0.0 110.9 %collective-permute-start = (bf16[1,1,2,64,2048]{4,3,2,1,0:T(8,128)(2,1)}, bf16[1,1,2,64,2048]{4,3,2,1,0:T(8,128)(2,1)S(1)}, u32[]{:S(2)}, u32[]{:S(2)}) collective-permute-start(bf16[1,1,2,64,2048]{4,3,2,1,0:T(8,128)(2,1)} %param.10), channel_id=1, source_target_pairs={{0,16},{16,32},{32,48},{48,64},{64,80},{80,96},{96,112},{112,128},... | collective-permute-start | bytes 1572872 | tf_op jit(solution)/shard_map/ppermute | solution.py:16
  3.6 112.2 %collective-permute-start.1 = (bf16[1,1,2,64,2048]{4,3,2,1,0:T(8,128)(2,1)}, bf16[1,1,2,64,2048]{4,3,2,1,0:T(8,128)(2,1)}, u32[]{:S(2)}, u32[]{:S(2)}) collective-permute-start(bf16[1,1,2,64,2048]{4,3,2,1,0:T(8,128)(2,1)} %param.10), channel_id=1, source_target_pairs={{16,0},{32,16},{48,32},{64,48},{80,64},{96,80},{112,96},{128,112},... | collective-permute-start | bytes 1572872 | tf_op jit(solution)/shard_map/ppermute | solution.py:19
  4.9 83.1 %collective-permute-start.5 = (bf16[1,1,1,32,2048]{4,3,2,1,0:T(8,128)(2,1)}, bf16[1,1,1,32,2048]{4,3,2,1,0:T(8,128)(2,1)}, u32[]{:S(2)}, u32[]{:S(2)}) collective-permute-start(bf16[1,1,1,32,2048]{4,3,2,1,0:T(8,128)(2,1)} %bitcast.214), channel_id=1, source_target_pairs={{16,0},{32,16},{48,32},{64,48},{80,64},{96,80},{112,96},{128,112},... | collective-permute-start | bytes 393224 | tf_op jit(solution)/shard_map/ppermute | solution.py:19
  6.2 89.8 %collective-permute-start.4 = (bf16[1,1,1,32,2048]{4,3,2,1,0:T(8,128)(2,1)}, bf16[1,1,1,32,2048]{4,3,2,1,0:T(8,128)(2,1)}, u32[]{:S(2)}, u32[]{:S(2)}) collective-permute-start(bf16[1,1,1,32,2048]{4,3,2,1,0:T(8,128)(2,1)} %bitcast.215), channel_id=1, source_target_pairs={{0,16},{16,32},{32,48},{48,64},{64,80},{80,96},{96,112},{112,128},... | collective-permute-start | bytes 393224 | tf_op jit(solution)/shard_map/ppermute | solution.py:16
  12.1 88.7 %collective-permute-start.13 = (bf16[1,1,1,32,2048]{4,3,2,1,0:T(8,128)(2,1)}, bf16[1,1,1,32,2048]{4,3,2,1,0:T(8,128)(2,1)S(1)}, u32[]{:S(2)}, u32[]{:S(2)}) collective-permute-start(bf16[1,1,1,32,2048]{4,3,2,1,0:T(8,128)(2,1)} %bitcast.218), channel_id=1, source_target_pairs={{16,0},{32,16},{48,32},{64,48},{80,64},{96,80},{112,96},{128,112},... | collective-permute-start | bytes 393224 | tf_op jit(solution)/shard_map/ppermute | solution.py:19
  88.1 14.0 %collective-permute-start.12 = (bf16[1,1,1,32,2048]{4,3,2,1,0:T(8,128)(2,1)S(1)}, bf16[1,1,1,32,2048]{4,3,2,1,0:T(8,128)(2,1)S(1)}, u32[]{:S(2)}, u32[]{:S(2)}) collective-permute-start(bf16[1,1,1,32,2048]{4,3,2,1,0:T(8,128)(2,1)S(1)} %bitcast.219), channel_id=1, source_target_pairs={{0,16},{16,32},{32,48},{48,64},{64,80},{80,96},{96,112},{112,128},... | collective-permute-start | bytes 393224 | tf_op jit(solution)/shard_map/ppermute | solution.py:16
  96.1 30.6 %collective-permute-start.8 = (bf16[1,1,2,64,2048]{4,3,2,1,0:T(8,128)(2,1)}, bf16[1,1,2,64,2048]{4,3,2,1,0:T(8,128)(2,1)S(1)}, u32[]{:S(2)}, u32[]{:S(2)}) collective-permute-start(bf16[1,1,2,64,2048]{4,3,2,1,0:T(8,128)(2,1)} %param.9), channel_id=1, source_target_pairs={{0,16},{16,32},{32,48},{48,64},{64,80},{80,96},{96,112},{112,128},... | collective-permute-start | bytes 1572872 | tf_op jit(solution)/shard_map/ppermute | solution.py:16
  100.8 43.1 %collective-permute-start.9 = (bf16[1,1,2,64,2048]{4,3,2,1,0:T(8,128)(2,1)}, bf16[1,1,2,64,2048]{4,3,2,1,0:T(8,128)(2,1)S(1)}, u32[]{:S(2)}, u32[]{:S(2)}) collective-permute-start(bf16[1,1,2,64,2048]{4,3,2,1,0:T(8,128)(2,1)} %param.9), channel_id=1, source_target_pairs={{16,0},{32,16},{48,32},{64,48},{80,64},{96,80},{112,96},{128,112},... | collective-permute-start | bytes 1572872 | tf_op jit(solution)/shard_map/ppermute | solution.py:19
  102.1 13.8 %copy-start.5 = (bf16[1,1,1,32,2048]{4,3,2,1,0:T(8,128)(2,1)}, bf16[1,1,1,32,2048]{4,3,2,1,0:T(8,128)(2,1)S(1)}, u32[]{:S(2)}) copy-start(bf16[1,1,1,32,2048]{4,3,2,1,0:T(8,128)(2,1)S(1)} %collective-permute-done.12) | copy-start | bytes 393220
  102.1 29.2 %collective-permute-start.7 = (bf16[1,3,1,32,2048]{4,3,2,1,0:T(8,128)(2,1)S(1)}, bf16[1,3,1,32,2048]{4,3,2,1,0:T(8,128)(2,1)S(1)}, u32[]{:S(2)}, u32[]{:S(2)}) collective-permute-start(bf16[1,3,1,32,2048]{4,3,2,1,0:T(8,128)(2,1)S(1)} %pad_maximum_fusion.3), channel_id=1, source_target_pairs={{1,0},{2,1},{3,2},{4,3},{5,4},{6,5},{7,6},{8,7},{9,8},{10,9},{11,1... | collective-permute-start | bytes 1179656 | tf_op jit(solution)/shard_map/ppermute | solution.py:19
  110.9 0.8 copy-start.2
  111.7 28.0 %collective-permute-start.6 = (bf16[1,3,1,32,2048]{4,3,2,1,0:T(8,128)(2,1)S(1)}, bf16[1,3,1,32,2048]{4,3,2,1,0:T(8,128)(2,1)S(1)}, u32[]{:S(2)}, u32[]{:S(2)}) collective-permute-start(bf16[1,3,1,32,2048]{4,3,2,1,0:T(8,128)(2,1)S(1)} %pad_maximum_fusion.3), channel_id=1, source_target_pairs={{0,1},{1,2},{2,3},{3,4},{4,5},{5,6},{6,7},{7,8},{8,9},{9,10},{10,1... | collective-permute-start | bytes 1179656 | tf_op jit(solution)/shard_map/ppermute | solution.py:16
  115.8 45.4 %collective-permute-start.15 = (bf16[1,3,1,32,2048]{4,3,2,1,0:T(8,128)(2,1)}, bf16[1,3,1,32,2048]{4,3,2,1,0:T(8,128)(2,1)}, u32[]{:S(2)}, u32[]{:S(2)}) collective-permute-start(bf16[1,3,1,32,2048]{4,3,2,1,0:T(8,128)(2,1)} %pad_maximum_fusion.2), channel_id=1, source_target_pairs={{1,0},{2,1},{3,2},{4,3},{5,4},{6,5},{7,6},{8,7},{9,8},{10,9},{11,1... | collective-permute-start | bytes 1179656 | tf_op jit(solution)/shard_map/ppermute | solution.py:19
  126.7 36.5 %collective-permute-start.14 = (bf16[1,3,1,32,2048]{4,3,2,1,0:T(8,128)(2,1)}, bf16[1,3,1,32,2048]{4,3,2,1,0:T(8,128)(2,1)}, u32[]{:S(2)}, u32[]{:S(2)}) collective-permute-start(bf16[1,3,1,32,2048]{4,3,2,1,0:T(8,128)(2,1)} %pad_maximum_fusion.2), channel_id=1, source_target_pairs={{0,1},{1,2},{2,3},{3,4},{4,5},{5,6},{6,7},{7,8},{8,9},{9,10},{10,1... | collective-permute-start | bytes 1179656 | tf_op jit(solution)/shard_map/ppermute | solution.py:16
  131.3 38.7 %collective-permute-start.3 = (bf16[1,3,1,64,2048]{4,3,2,1,0:T(8,128)(2,1)}, bf16[1,3,1,64,2048]{4,3,2,1,0:T(8,128)(2,1)}, u32[]{:S(2)}, u32[]{:S(2)}) collective-permute-start(bf16[1,3,1,64,2048]{4,3,2,1,0:T(8,128)(2,1)} %get-tuple-element.59), channel_id=1, source_target_pairs={{1,0},{2,1},{3,2},{4,3},{5,4},{6,5},{7,6},{8,7},{9,8},{10,9},{11,1... | collective-permute-start | bytes 2359304 | tf_op jit(solution)/shard_map/ppermute | solution.py:19
  139.8 69.3 %collective-permute-start.2 = (bf16[1,3,1,64,2048]{4,3,2,1,0:T(8,128)(2,1)}, bf16[1,3,1,64,2048]{4,3,2,1,0:T(8,128)(2,1)}, u32[]{:S(2)}, u32[]{:S(2)}) collective-permute-start(bf16[1,3,1,64,2048]{4,3,2,1,0:T(8,128)(2,1)} %get-tuple-element.58), channel_id=1, source_target_pairs={{0,1},{1,2},{2,3},{3,4},{4,5},{5,6},{6,7},{7,8},{8,9},{9,10},{10,1... | collective-permute-start | bytes 2359304 | tf_op jit(solution)/shard_map/ppermute | solution.py:16
  152.8 60.1 %collective-permute-start.11 = (bf16[1,3,1,64,2048]{4,3,2,1,0:T(8,128)(2,1)}, bf16[1,3,1,64,2048]{4,3,2,1,0:T(8,128)(2,1)}, u32[]{:S(2)}, u32[]{:S(2)}) collective-permute-start(bf16[1,3,1,64,2048]{4,3,2,1,0:T(8,128)(2,1)} %get-tuple-element.57), channel_id=1, source_target_pairs={{1,0},{2,1},{3,2},{4,3},{5,4},{6,5},{7,6},{8,7},{9,8},{10,9},{11,1... | collective-permute-start | bytes 2359304 | tf_op jit(solution)/shard_map/ppermute | solution.py:19
  161.3 62.3 %collective-permute-start.10 = (bf16[1,3,1,64,2048]{4,3,2,1,0:T(8,128)(2,1)}, bf16[1,3,1,64,2048]{4,3,2,1,0:T(8,128)(2,1)}, u32[]{:S(2)}, u32[]{:S(2)}) collective-permute-start(bf16[1,3,1,64,2048]{4,3,2,1,0:T(8,128)(2,1)} %get-tuple-element.56), channel_id=1, source_target_pairs={{0,1},{1,2},{2,3},{3,4},{4,5},{5,6},{6,7},{7,8},{8,9},{9,10},{10,1... | collective-permute-start | bytes 2359304 | tf_op jit(solution)/shard_map/ppermute | solution.py:16
  227.7 1.9 copy-start.6
  233.9 2.2 copy-start
  236.4 2.2 copy-start.1
where the time goes:
time: 242 us; the launch traced here: 241 us
  starting transfers between devices  67.3 us (28%)
  blocking collectives  63 us (26%)
  waiting for transfers between devices  49.9 us (21%)
  local copies, waits for them, and re-layouts  38.1 us (16%)
  other arithmetic  16.2 us (7%)
  matrix products  5.78 us (2%)
    ppermute x8, waiting for transfers between devices, extended(): lax.ppermute(lax.slice_in_dim(block, block.shape[dim] - width, None, axis...  49.9 us
    ppermute x8, starting transfers between devices, extended(): lax.ppermute(lax.slice_in_dim(block, 0, width, axis=dim), axis, backward)  38.5 us
    all_gather x1, blocking collectives, body(): lax.all_gather(top_keys, 'col', axis=1, tiled=True)  35.2 us
    ppermute x8, starting transfers between devices, extended(): lax.ppermute(lax.slice_in_dim(block, block.shape[dim] - width, None, axis...  28.8 us
    all_gather x1, blocking collectives, body(): lax.all_gather(top_values, 'col', axis=1, tiled=True)  27.7 us
    unnamed x57, local copies, waits for them, and re-layouts  15.8 us
    concatenate x4, other arithmetic, extended(): block = jnp.concatenate([low, block, high], axis=dim)  6.27 us
  transfers between devices with their start and end apart: 16, of which 2 were waited for; matrix products, arithmetic and copies ran while one was open for 18% of the time, Pallas kernels for 0%

commit v1 on v0

--- a/solution.py
+++ b/solution.py
@@ -3,6 +3,7 @@
 import jax.numpy as jnp
 from jax import lax
 from jax.sharding import PartitionSpec as P
+from jax.lax import all_to_all, axis_size
 
 HEADS = 16
 NEG_FILL = -1e30
@@ -45,7 +46,10 @@
     around_keys = around_keys.reshape(9 * pool_blocks, pool_tokens, model_width)
     around_values = around_values.reshape(9 * pool_blocks, pool_tokens, model_width)
     top_all_keys, top_all_values = (
-        lax.all_gather(top_keys, "col", axis=1, tiled=True),
+        jnp.concatenate(
+            all_to_all(jnp.stack([top_keys for _ in range(axis_size("col"))], 0), "col", 0, 0),
+            axis=1,
+        ),
         lax.all_gather(top_values, "col", axis=1, tiled=True),
     )
     owner_device = coarse_ids // pool_blocks

time: 242 us -> 222 us (0.917)
  the two profiles are of different devices: /device:TPU:6 before, /device:TPU:4 now
where the time goes in v1:
time: 222 us; the launch traced here: 221 us
  starting transfers between devices  77 us (35%)
  waiting for transfers between devices  56.1 us (25%)
  blocking collectives  34.8 us (16%)
  local copies, waits for them, and re-layouts  32.5 us (15%)
  other arithmetic  12.4 us (6%)
  matrix products  7.01 us (3%)
    ppermute x8, starting transfers between devices, extended(): lax.ppermute(lax.slice_in_dim(block, 0, width, axis=dim), axis, backward)  36.7 us
    all_gather x1, blocking collectives, body(): lax.all_gather(top_values, 'col', axis=1, tiled=True)  34.8 us
    ppermute x8, waiting for transfers between devices, extended(): lax.ppermute(lax.slice_in_dim(block, block.shape[dim] - width, None, axis...  32.3 us
    ppermute x8, starting transfers between devices, extended(): lax.ppermute(lax.slice_in_dim(block, block.shape[dim] - width, None, axis...  27 us
    ppermute x8, waiting for transfers between devices, extended(): lax.ppermute(lax.slice_in_dim(block, 0, width, axis=dim), axis, backward)  23.8 us
    unnamed x70, local copies, waits for them, and re-layouts  15.1 us
    all_to_all x1, starting transfers between devices, body(): all_to_all(jnp.stack([top_keys for _ in range(axis_size('col'))], 0), 'co...  13.3 us
    concatenate x4, other arithmetic, extended(): block = jnp.concatenate([low, block, high], axis=dim)  5.24 us
  transfers between devices with their start and end apart: 17, of which 6 were waited for; matrix products, arithmetic and copies ran while one was open for 16% of the time, Pallas kernels for 0%

profile of v1, /device:TPU:4, one launch (start us, length us, event | category | flops | bytes accessed | tf_op | source)
XLA Modules:
  0.0 220.6 jit_solution(2684121386810606569)
XLA Ops:
  0.0 3.6 %collective-permute-start = (bf16[1,1,2,64,2048]{4,3,2,1,0:T(8,128)(2,1)}, bf16[1,1,2,64,2048]{4,3,2,1,0:T(8,128)(2,1)S(1)}, u32[]{:S(2)}, u32[]{:S(2)}) collective-permute-start(bf16[1,1,2,64,2048]{4,3,2,1,0:T(8,128)(2,1)} %param.10), channel_id=1, source_target_pairs={{0,16},{16,32},{32,48},{48,64},{64,80},{80,96},{96,112},{112,128},... | collective-permute-start | bytes 1572872 | tf_op jit(solution)/shard_map/ppermute | solution.py:17
  3.6 1.3 collective-permute-start.1
  4.9 1.3 collective-permute-start.5
  6.2 5.2 %collective-permute-start.4 = (bf16[1,1,1,32,2048]{4,3,2,1,0:T(8,128)(2,1)}, bf16[1,1,1,32,2048]{4,3,2,1,0:T(8,128)(2,1)S(1)}, u32[]{:S(2)}, u32[]{:S(2)}) collective-permute-start(bf16[1,1,1,32,2048]{4,3,2,1,0:T(8,128)(2,1)} %bitcast.218), channel_id=1, source_target_pairs={{0,16},{16,32},{32,48},{48,64},{64,80},{80,96},{96,112},{112,128},... | collective-permute-start | bytes 393224 | tf_op jit(solution)/shard_map/ppermute | solution.py:17
  11.4 1.3 collective-permute-start.13
  12.7 1.7 stack.2
  14.4 13.3 %all-to-all-start = ((bf16[16,1,8,2048]{3,2,1,0:T(8,128)(2,1)}), bf16[16,1,8,2048]{3,2,1,0:T(8,128)(2,1)}, u32[]{:S(2)}, u32[]{:S(2)}) async-start(bf16[16,1,8,2048]{3,2,1,0:T(8,128)(2,1)} %stack.2), calls=%async_computation | async-start | bytes 1048576 | tf_op jit(solution)/shard_map/all_to_all | solution.py:50
  27.7 0.7 compare_select_fusion
  28.5 34.8 %all_gather.3 = bf16[1,128,2048]{2,1,0:T(8,128)(2,1)S(1)} all-gather(bf16[1,8,2048]{2,1,0:T(8,128)(2,1)} %param.14), channel_id=1, replica_groups=mesh['row'=32,'col'=16] {'col'}, dimensions={1}, use_global_device_ids=true | all-gather | bytes 557056 | tf_op jit(solution)/shard_map/all_gather | solution.py:53
  63.3 1.1 copy.115
  64.5 0.8 copy-done
  65.3 1.0 copy.94
  66.2 1.0 copy.99
  68.0 3.6 %collective-permute-start.12 = (bf16[1,1,1,32,2048]{4,3,2,1,0:T(8,128)(2,1)}, bf16[1,1,1,32,2048]{4,3,2,1,0:T(8,128)(2,1)S(1)}, u32[]{:S(2)}, u32[]{:S(2)}) collective-permute-start(bf16[1,1,1,32,2048]{4,3,2,1,0:T(8,128)(2,1)} %bitcast.222), channel_id=1, source_target_pairs={{0,16},{16,32},{32,48},{48,64},{64,80},{80,96},{96,112},{112,128},... | collective-permute-start | bytes 393224 | tf_op jit(solution)/shard_map/ppermute | solution.py:17
  71.7 4.0 %collective-permute-start.8 = (bf16[1,1,2,64,2048]{4,3,2,1,0:T(8,128)(2,1)}, bf16[1,1,2,64,2048]{4,3,2,1,0:T(8,128)(2,1)S(1)}, u32[]{:S(2)}, u32[]{:S(2)}) collective-permute-start(bf16[1,1,2,64,2048]{4,3,2,1,0:T(8,128)(2,1)} %param.9), channel_id=1, source_target_pairs={{0,16},{16,32},{32,48},{48,64},{64,80},{80,96},{96,112},{112,128},... | collective-permute-start | bytes 1572872 | tf_op jit(solution)/shard_map/ppermute | solution.py:17
  75.6 1.0 pad_maximum_fusion.3
  76.6 1.3 collective-permute-start.9
  77.9 8.9 %collective-permute-start.7 = (bf16[1,3,1,32,2048]{4,3,2,1,0:T(8,128)(2,1)S(1)}, bf16[1,3,1,32,2048]{4,3,2,1,0:T(8,128)(2,1)S(1)}, u32[]{:S(2)}, u32[]{:S(2)}) collective-permute-start(bf16[1,3,1,32,2048]{4,3,2,1,0:T(8,128)(2,1)S(1)} %pad_maximum_fusion.3), channel_id=1, source_target_pairs={{1,0},{2,1},{3,2},{4,3},{5,4},{6,5},{7,6},{8,7},{9,8},{10,9},{11,1... | collective-permute-start | bytes 1179656 | tf_op jit(solution)/shard_map/ppermute | solution.py:20
  86.8 0.8 pad_maximum_fusion.2
  87.6 1.9 collective-permute-start.6
  89.7 8.4 %collective-permute-start.15 = (bf16[1,3,1,32,2048]{4,3,2,1,0:T(8,128)(2,1)}, bf16[1,3,1,32,2048]{4,3,2,1,0:T(8,128)(2,1)}, u32[]{:S(2)}, u32[]{:S(2)}) collective-permute-start(bf16[1,3,1,32,2048]{4,3,2,1,0:T(8,128)(2,1)} %pad_maximum_fusion.2), channel_id=1, source_target_pairs={{1,0},{2,1},{3,2},{4,3},{5,4},{6,5},{7,6},{8,7},{9,8},{10,9},{11,1... | collective-permute-start | bytes 1179656 | tf_op jit(solution)/shard_map/ppermute | solution.py:20
  98.2 1.1 constant_dynamic-update-slice_fusion.1
  99.3 1.9 collective-permute-start.14
  101.2 1.1 constant_dynamic-update-slice_fusion.3
  102.3 1.2 fusion.21
  103.6 8.4 %collective-permute-start.3 = (bf16[1,3,1,64,2048]{4,3,2,1,0:T(8,128)(2,1)}, bf16[1,3,1,64,2048]{4,3,2,1,0:T(8,128)(2,1)}, u32[]{:S(2)}, u32[]{:S(2)}) collective-permute-start(bf16[1,3,1,64,2048]{4,3,2,1,0:T(8,128)(2,1)} %get-tuple-element.59), channel_id=1, source_target_pairs={{1,0},{2,1},{3,2},{4,3},{5,4},{6,5},{7,6},{8,7},{9,8},{10,9},{11,1... | collective-permute-start | bytes 2359304 | tf_op jit(solution)/shard_map/ppermute | solution.py:20
  112.1 1.3 fusion.20
  113.4 11.0 %collective-permute-done.7 = bf16[1,3,1,32,2048]{4,3,2,1,0:T(8,128)(2,1)S(1)} collective-permute-done((bf16[1,3,1,32,2048]{4,3,2,1,0:T(8,128)(2,1)S(1)}, bf16[1,3,1,32,2048]{4,3,2,1,0:T(8,128)(2,1)S(1)}, u32[]{:S(2)}, u32[]{:S(2)}) %collective-permute-start.7) | collective-permute-done | bytes 393248 | tf_op jit(solution)/shard_map/ppermute | solution.py:20
  124.4 4.9 %collective-permute-start.2 = (bf16[1,3,1,64,2048]{4,3,2,1,0:T(8,128)(2,1)}, bf16[1,3,1,64,2048]{4,3,2,1,0:T(8,128)(2,1)}, u32[]{:S(2)}, u32[]{:S(2)}) collective-permute-start(bf16[1,3,1,64,2048]{4,3,2,1,0:T(8,128)(2,1)} %get-tuple-element.58), channel_id=1, source_target_pairs={{0,1},{1,2},{2,3},{3,4},{4,5},{5,6},{6,7},{7,8},{8,9},{9,10},{10,1... | collective-permute-start | bytes 2359304 | tf_op jit(solution)/shard_map/ppermute | solution.py:17
  129.3 1.2 pad_maximum_fusion.1
  130.4 2.9 %gather_fusion = bf16[16,16,2048]{2,1,0:T(8,128)(2,1)} fusion(bf16[18,16,2048]{2,1,0:T(8,128)(2,1)} %bitcast.172, s32[1024]{0:T(1024)S(1)} %pad_clamp_fusion), kind=kCustom, calls=%fused_computation | custom fusion | bytes 2097216 | tf_op jit(solution)/shard_map/while/body/eval_jaxpr/gather | solution.py:97
  133.3 2.5 %copy.126 = bf16[32,8,16,128]{3,2,1,0:T(8,128)(2,1)} copy(bf16[32,8,16,128]{3,1,2,0:T(8,128)(2,1)} %bitcast.176) | data formatting | bytes 2097152
  135.8 5.8 %collective-permute-start.11 = (bf16[1,3,1,64,2048]{4,3,2,1,0:T(8,128)(2,1)}, bf16[1,3,1,64,2048]{4,3,2,1,0:T(8,128)(2,1)}, u32[]{:S(2)}, u32[]{:S(2)}) collective-permute-start(bf16[1,3,1,64,2048]{4,3,2,1,0:T(8,128)(2,1)} %get-tuple-element.57), channel_id=1, source_target_pairs={{1,0},{2,1},{3,2},{4,3},{5,4},{6,5},{7,6},{8,7},{9,8},{10,9},{11,1... | collective-permute-start | bytes 2359304 | tf_op jit(solution)/shard_map/ppermute | solution.py:20
  141.6 1.9 collective-permute-start.10
  143.5 0.6 collective-permute-done.14
  144.2 2.3 %pad_maximum_fusion = bf16[1,3,3,32,2048]{4,3,2,1,0:T(8,128)(2,1)} fusion(bf16[1,3,1,32,2048]{4,3,2,1,0:T(8,128)(2,1)} %collective-permute-done.15, bf16[1,1,1,32,2048]{4,3,2,1,0:T(8,128)(2,1)S(1)} %collective-permute-done.13, bf16[1,1,1,32,2048]{4,3,2,1,0:T(8,128)(2,1)S(1)} %bitcast.224, bf16[1,1,1,32,2048]{4,3,2,1,0:T(8,128)(2,1)} %copy-done.10, ...), kind=kLoop, calls=%fused_computation.16 | loop fusion | flops 2359296 | bytes 2359296 | tf_op jit(solution)/shard_map/concatenate | solution.py:21
  146.5 2.9 %gather_fusion.1 = bf16[16,16,2048]{2,1,0:T(8,128)(2,1)} fusion(bf16[18,16,2048]{2,1,0:T(8,128)(2,1)} %bitcast.171, s32[1024]{0:T(1024)S(1)} %pad_clamp_fusion), kind=kCustom, calls=%fused_computation.1 | custom fusion | bytes 2097216 | tf_op jit(solution)/shard_map/while/body/eval_jaxpr/gather | solution.py:96
  149.4 2.4 %copy.114 = bf16[32,8,16,128]{3,2,1,0:T(8,128)(2,1)} copy(bf16[32,8,16,128]{3,1,2,0:T(8,128)(2,1)} %bitcast.175) | data formatting | bytes 2097152
  151.8 1.1 copy.116
  152.9 1.5 fusion.10
  154.5 0.4 bitcast_reduce_fusion.1
  154.8 6.7 %collective-permute-done.3 = bf16[1,3,1,64,2048]{4,3,2,1,0:T(8,128)(2,1)} collective-permute-done((bf16[1,3,1,64,2048]{4,3,2,1,0:T(8,128)(2,1)}, bf16[1,3,1,64,2048]{4,3,2,1,0:T(8,128)(2,1)}, u32[]{:S(2)}, u32[]{:S(2)}) %collective-permute-start.3) | collective-permute-done | bytes 786464 | tf_op jit(solution)/shard_map/ppermute | solution.py:20
  161.5 16.6 %collective-permute-done.2 = bf16[1,3,1,64,2048]{4,3,2,1,0:T(8,128)(2,1)} collective-permute-done((bf16[1,3,1,64,2048]{4,3,2,1,0:T(8,128)(2,1)}, bf16[1,3,1,64,2048]{4,3,2,1,0:T(8,128)(2,1)}, u32[]{:S(2)}, u32[]{:S(2)}) %collective-permute-start.2) | collective-permute-done | bytes 786464 | tf_op jit(solution)/shard_map/ppermute | solution.py:17
  178.1 1.7 maximum_bitcast_fusion.1
  179.8 0.6 fusion.19
  181.5 1.0 copy_dynamic-update-slice_fusion.19
  182.5 6.1 %collective-permute-done.11 = bf16[1,3,1,64,2048]{4,3,2,1,0:T(8,128)(2,1)} collective-permute-done((bf16[1,3,1,64,2048]{4,3,2,1,0:T(8,128)(2,1)}, bf16[1,3,1,64,2048]{4,3,2,1,0:T(8,128)(2,1)}, u32[]{:S(2)}, u32[]{:S(2)}) %collective-permute-start.11) | collective-permute-done | bytes 786464 | tf_op jit(solution)/shard_map/ppermute | solution.py:20
  188.6 15.1 %collective-permute-done.10 = bf16[1,3,1,64,2048]{4,3,2,1,0:T(8,128)(2,1)} collective-permute-done((bf16[1,3,1,64,2048]{4,3,2,1,0:T(8,128)(2,1)}, bf16[1,3,1,64,2048]{4,3,2,1,0:T(8,128)(2,1)}, u32[]{:S(2)}, u32[]{:S(2)}) %collective-permute-start.10) | collective-permute-done | bytes 786464 | tf_op jit(solution)/shard_map/ppermute | solution.py:17
  203.7 1.7 maximum_bitcast_fusion
  205.4 0.8 fusion.18
  207.5 0.2 copy_dynamic-update-slice_fusion.9
  208.9 0.3 copy_dynamic-update-slice_fusion
  209.3 2.3 %bitcast_reduce_fusion = (f32[2,16,64]{2,1,0:T(8,128)S(1)}, f32[2,16,704,64]{2,3,1,0:T(8,128)S(1)}) fusion(pred[2,704]{1,0:T(4,128)(4,1)S(1)} %concatenate.92, bf16[2,704,16,128]{3,1,2,0:T(8,128)(2,1)S(1)} %copy_dynamic-update-slice_fusion, bf16[2,64,16,128]{3,2,1,0:T(8,128)(2,1)S(1)} %bitcast.170), kind=kOutput, calls=%fused_computation.3 | convolution fusion | flops 373422080 | bytes 12068224 | tf_op jit(solution)/shard_map/while/body/eval_jaxpr/bqhd,bkhd->bhqk/dot_general | solution.py:103
  211.7 1.9 fusion.1
  213.6 0.7 fusion.8
  214.7 0.2 copy_dynamic-update-slice_fusion.16
  214.8 0.2 copy_dynamic-update-slice_fusion.15
  215.0 0.2 copy_dynamic-update-slice_fusion.14
  215.2 0.2 copy_dynamic-update-slice_fusion.13
  215.7 0.3 copy_dynamic-update-slice_fusion.1
  216.1 2.2 fusion.4
  218.3 1.0 fusion.6
  219.3 0.3 copy.102
  219.6 1.0 convert_element_type.27
  (93 shorter events, 5.2 us)
Async XLA Ops:
  0.0 89.6 %copy-start.4 = (bf16[1,1,2,64,2048]{4,3,2,1,0:T(8,128)(2,1)S(1)}, bf16[1,1,2,64,2048]{4,3,2,1,0:T(8,128)(2,1)}, u32[]{:S(2)}) copy-start(bf16[1,1,2,64,2048]{4,3,2,1,0:T(8,128)(2,1)} %param.10) | copy-start | bytes 1572868
  0.0 86.8 %copy-start.7 = (bf16[2,16,2048]{2,1,0:T(8,128)(2,1)S(1)}, bf16[2,16,2048]{2,1,0:T(8,128)(2,1)}, u32[]{:S(2)}) copy-start(bf16[2,16,2048]{2,1,0:T(8,128)(2,1)} %param.11) | copy-start | bytes 393220
  0.0 87.6 %collective-permute-start = (bf16[1,1,2,64,2048]{4,3,2,1,0:T(8,128)(2,1)}, bf16[1,1,2,64,2048]{4,3,2,1,0:T(8,128)(2,1)S(1)}, u32[]{:S(2)}, u32[]{:S(2)}) collective-permute-start(bf16[1,1,2,64,2048]{4,3,2,1,0:T(8,128)(2,1)} %param.10), channel_id=1, source_target_pairs={{0,16},{16,32},{32,48},{48,64},{64,80},{80,96},{96,112},{112,128},... | collective-permute-start | bytes 1572872 | tf_op jit(solution)/shard_map/ppermute | solution.py:17
  3.6 95.7 %collective-permute-start.1 = (bf16[1,1,2,64,2048]{4,3,2,1,0:T(8,128)(2,1)}, bf16[1,1,2,64,2048]{4,3,2,1,0:T(8,128)(2,1)}, u32[]{:S(2)}, u32[]{:S(2)}) collective-permute-start(bf16[1,1,2,64,2048]{4,3,2,1,0:T(8,128)(2,1)} %param.10), channel_id=1, source_target_pairs={{16,0},{32,16},{48,32},{64,48},{80,64},{96,80},{112,96},{128,112},... | collective-permute-start | bytes 1572872 | tf_op jit(solution)/shard_map/ppermute | solution.py:20
  4.9 63.1 %collective-permute-start.5 = (bf16[1,1,1,32,2048]{4,3,2,1,0:T(8,128)(2,1)}, bf16[1,1,1,32,2048]{4,3,2,1,0:T(8,128)(2,1)S(1)}, u32[]{:S(2)}, u32[]{:S(2)}) collective-permute-start(bf16[1,1,1,32,2048]{4,3,2,1,0:T(8,128)(2,1)} %bitcast.217), channel_id=1, source_target_pairs={{16,0},{32,16},{48,32},{64,48},{80,64},{96,80},{112,96},{128,112},... | collective-permute-start | bytes 393224 | tf_op jit(solution)/shard_map/ppermute | solution.py:20
  6.2 65.4 %collective-permute-start.4 = (bf16[1,1,1,32,2048]{4,3,2,1,0:T(8,128)(2,1)}, bf16[1,1,1,32,2048]{4,3,2,1,0:T(8,128)(2,1)S(1)}, u32[]{:S(2)}, u32[]{:S(2)}) collective-permute-start(bf16[1,1,1,32,2048]{4,3,2,1,0:T(8,128)(2,1)} %bitcast.218), channel_id=1, source_target_pairs={{0,16},{16,32},{32,48},{48,64},{64,80},{80,96},{96,112},{112,128},... | collective-permute-start | bytes 393224 | tf_op jit(solution)/shard_map/ppermute | solution.py:17
  11.4 65.2 %collective-permute-start.13 = (bf16[1,1,1,32,2048]{4,3,2,1,0:T(8,128)(2,1)}, bf16[1,1,1,32,2048]{4,3,2,1,0:T(8,128)(2,1)S(1)}, u32[]{:S(2)}, u32[]{:S(2)}) collective-permute-start(bf16[1,1,1,32,2048]{4,3,2,1,0:T(8,128)(2,1)} %bitcast.221), channel_id=1, source_target_pairs={{16,0},{32,16},{48,32},{64,48},{80,64},{96,80},{112,96},{128,112},... | collective-permute-start | bytes 393224 | tf_op jit(solution)/shard_map/ppermute | solution.py:20
  14.4 137.4 %all-to-all-start = ((bf16[16,1,8,2048]{3,2,1,0:T(8,128)(2,1)}), bf16[16,1,8,2048]{3,2,1,0:T(8,128)(2,1)}, u32[]{:S(2)}, u32[]{:S(2)}) async-start(bf16[16,1,8,2048]{3,2,1,0:T(8,128)(2,1)} %stack.2), calls=%async_computation | async-start | bytes 1048576 | tf_op jit(solution)/shard_map/all_to_all | solution.py:50
  64.5 0.8 copy-start
  68.0 9.9 %collective-permute-start.12 = (bf16[1,1,1,32,2048]{4,3,2,1,0:T(8,128)(2,1)}, bf16[1,1,1,32,2048]{4,3,2,1,0:T(8,128)(2,1)S(1)}, u32[]{:S(2)}, u32[]{:S(2)}) collective-permute-start(bf16[1,1,1,32,2048]{4,3,2,1,0:T(8,128)(2,1)} %bitcast.222), channel_id=1, source_target_pairs={{0,16},{16,32},{32,48},{48,64},{64,80},{80,96},{96,112},{112,128},... | collective-permute-start | bytes 393224 | tf_op jit(solution)/shard_map/ppermute | solution.py:17
  71.7 18.0 %copy-start.8 = (bf16[1,1,1,32,2048]{4,3,2,1,0:T(8,128)(2,1)}, bf16[1,1,1,32,2048]{4,3,2,1,0:T(8,128)(2,1)S(1)}, u32[]{:S(2)}) copy-start(bf16[1,1,1,32,2048]{4,3,2,1,0:T(8,128)(2,1)S(1)} %collective-permute-done.4) | copy-start | bytes 393220
  71.7 18.0 %collective-permute-start.8 = (bf16[1,1,2,64,2048]{4,3,2,1,0:T(8,128)(2,1)}, bf16[1,1,2,64,2048]{4,3,2,1,0:T(8,128)(2,1)S(1)}, u32[]{:S(2)}, u32[]{:S(2)}) collective-permute-start(bf16[1,1,2,64,2048]{4,3,2,1,0:T(8,128)(2,1)} %param.9), channel_id=1, source_target_pairs={{0,16},{16,32},{32,48},{48,64},{64,80},{80,96},{96,112},{112,128},... | collective-permute-start | bytes 1572872 | tf_op jit(solution)/shard_map/ppermute | solution.py:17
  76.6 27.0 %collective-permute-start.9 = (bf16[1,1,2,64,2048]{4,3,2,1,0:T(8,128)(2,1)}, bf16[1,1,2,64,2048]{4,3,2,1,0:T(8,128)(2,1)S(1)}, u32[]{:S(2)}, u32[]{:S(2)}) collective-permute-start(bf16[1,1,2,64,2048]{4,3,2,1,0:T(8,128)(2,1)} %param.9), channel_id=1, source_target_pairs={{16,0},{32,16},{48,32},{64,48},{80,64},{96,80},{112,96},{128,112},... | collective-permute-start | bytes 1572872 | tf_op jit(solution)/shard_map/ppermute | solution.py:20
  77.9 11.7 %copy-start.10 = (bf16[1,1,1,32,2048]{4,3,2,1,0:T(8,128)(2,1)}, bf16[1,1,1,32,2048]{4,3,2,1,0:T(8,128)(2,1)S(1)}, u32[]{:S(2)}) copy-start(bf16[1,1,1,32,2048]{4,3,2,1,0:T(8,128)(2,1)S(1)} %collective-permute-done.12) | copy-start | bytes 393220
  77.9 46.5 %collective-permute-start.7 = (bf16[1,3,1,32,2048]{4,3,2,1,0:T(8,128)(2,1)S(1)}, bf16[1,3,1,32,2048]{4,3,2,1,0:T(8,128)(2,1)S(1)}, u32[]{:S(2)}, u32[]{:S(2)}) collective-permute-start(bf16[1,3,1,32,2048]{4,3,2,1,0:T(8,128)(2,1)S(1)} %pad_maximum_fusion.3), channel_id=1, source_target_pairs={{1,0},{2,1},{3,2},{4,3},{5,4},{6,5},{7,6},{8,7},{9,8},{10,9},{11,1... | collective-permute-start | bytes 1179656 | tf_op jit(solution)/shard_map/ppermute | solution.py:20
  87.6 41.6 %collective-permute-start.6 = (bf16[1,3,1,32,2048]{4,3,2,1,0:T(8,128)(2,1)S(1)}, bf16[1,3,1,32,2048]{4,3,2,1,0:T(8,128)(2,1)S(1)}, u32[]{:S(2)}, u32[]{:S(2)}) collective-permute-start(bf16[1,3,1,32,2048]{4,3,2,1,0:T(8,128)(2,1)S(1)} %pad_maximum_fusion.3), channel_id=1, source_target_pairs={{0,1},{1,2},{2,3},{3,4},{4,5},{5,6},{6,7},{7,8},{8,9},{9,10},{10,1... | collective-permute-start | bytes 1179656 | tf_op jit(solution)/shard_map/ppermute | solution.py:17
  89.6 39.7 %copy-start.6 = (bf16[2,16,2048]{2,1,0:T(8,128)(2,1)S(1)}, bf16[2,16,2048]{2,1,0:T(8,128)(2,1)}, u32[]{:S(2)}) copy-start(bf16[2,16,2048]{2,1,0:T(8,128)(2,1)} %param.12) | copy-start | bytes 393220
  89.7 51.9 %collective-permute-start.15 = (bf16[1,3,1,32,2048]{4,3,2,1,0:T(8,128)(2,1)}, bf16[1,3,1,32,2048]{4,3,2,1,0:T(8,128)(2,1)}, u32[]{:S(2)}, u32[]{:S(2)}) collective-permute-start(bf16[1,3,1,32,2048]{4,3,2,1,0:T(8,128)(2,1)} %pad_maximum_fusion.2), channel_id=1, source_target_pairs={{1,0},{2,1},{3,2},{4,3},{5,4},{6,5},{7,6},{8,7},{9,8},{10,9},{11,1... | collective-permute-start | bytes 1179656 | tf_op jit(solution)/shard_map/ppermute | solution.py:20
  98.1 31.1 %copy-start.9 = (bf16[1,1,1,32,2048]{4,3,2,1,0:T(8,128)(2,1)S(1)}, bf16[1,1,1,32,2048]{4,3,2,1,0:T(8,128)(2,1)}, u32[]{:S(2)}) copy-start(bf16[1,1,1,32,2048]{4,3,2,1,0:T(8,128)(2,1)} %copy-done.8) | copy-start | bytes 393220
  99.3 44.8 %collective-permute-start.14 = (bf16[1,3,1,32,2048]{4,3,2,1,0:T(8,128)(2,1)}, bf16[1,3,1,32,2048]{4,3,2,1,0:T(8,128)(2,1)}, u32[]{:S(2)}, u32[]{:S(2)}) collective-permute-start(bf16[1,3,1,32,2048]{4,3,2,1,0:T(8,128)(2,1)} %pad_maximum_fusion.2), channel_id=1, source_target_pairs={{0,1},{1,2},{2,3},{3,4},{4,5},{5,6},{6,7},{7,8},{8,9},{9,10},{10,1... | collective-permute-start | bytes 1179656 | tf_op jit(solution)/shard_map/ppermute | solution.py:17
  103.6 57.9 %collective-permute-start.3 = (bf16[1,3,1,64,2048]{4,3,2,1,0:T(8,128)(2,1)}, bf16[1,3,1,64,2048]{4,3,2,1,0:T(8,128)(2,1)}, u32[]{:S(2)}, u32[]{:S(2)}) collective-permute-start(bf16[1,3,1,64,2048]{4,3,2,1,0:T(8,128)(2,1)} %get-tuple-element.59), channel_id=1, source_target_pairs={{1,0},{2,1},{3,2},{4,3},{5,4},{6,5},{7,6},{8,7},{9,8},{10,9},{11,1... | collective-permute-start | bytes 2359304 | tf_op jit(solution)/shard_map/ppermute | solution.py:20
  124.4 53.7 %collective-permute-start.2 = (bf16[1,3,1,64,2048]{4,3,2,1,0:T(8,128)(2,1)}, bf16[1,3,1,64,2048]{4,3,2,1,0:T(8,128)(2,1)}, u32[]{:S(2)}, u32[]{:S(2)}) collective-permute-start(bf16[1,3,1,64,2048]{4,3,2,1,0:T(8,128)(2,1)} %get-tuple-element.58), channel_id=1, source_target_pairs={{0,1},{1,2},{2,3},{3,4},{4,5},{5,6},{6,7},{7,8},{8,9},{9,10},{10,1... | collective-permute-start | bytes 2359304 | tf_op jit(solution)/shard_map/ppermute | solution.py:17
  135.8 52.8 %collective-permute-start.11 = (bf16[1,3,1,64,2048]{4,3,2,1,0:T(8,128)(2,1)}, bf16[1,3,1,64,2048]{4,3,2,1,0:T(8,128)(2,1)}, u32[]{:S(2)}, u32[]{:S(2)}) collective-permute-start(bf16[1,3,1,64,2048]{4,3,2,1,0:T(8,128)(2,1)} %get-tuple-element.57), channel_id=1, source_target_pairs={{1,0},{2,1},{3,2},{4,3},{5,4},{6,5},{7,6},{8,7},{9,8},{10,9},{11,1... | collective-permute-start | bytes 2359304 | tf_op jit(solution)/shard_map/ppermute | solution.py:20
  141.6 62.1 %collective-permute-start.10 = (bf16[1,3,1,64,2048]{4,3,2,1,0:T(8,128)(2,1)}, bf16[1,3,1,64,2048]{4,3,2,1,0:T(8,128)(2,1)}, u32[]{:S(2)}, u32[]{:S(2)}) collective-permute-start(bf16[1,3,1,64,2048]{4,3,2,1,0:T(8,128)(2,1)} %get-tuple-element.56), channel_id=1, source_target_pairs={{0,1},{1,2},{2,3},{3,4},{4,5},{5,6},{6,7},{7,8},{8,9},{9,10},{10,1... | collective-permute-start | bytes 2359304 | tf_op jit(solution)/shard_map/ppermute | solution.py:17
  207.1 1.8 copy-start.3
  207.3 1.9 copy-start.1
  208.9 5.4 %slice-start = ((s8[5767168]{0:T(1024)(128)(4,1)}), s8[4194304]{0:T(1024)(128)(4,1)S(1)}, s32[]{:S(2)}) async-start(s8[5767168]{0:T(1024)(128)(4,1)} %bitcast.225), calls=%async_computation.1 | async-start | bytes 8388608
  209.3 5.0 %slice-start.1 = ((s8[5767168]{0:T(1024)(128)(4,1)}), s8[1572864]{0:T(1024)(128)(4,1)S(1)}, s32[]{:S(2)}) async-start(s8[5767168]{0:T(1024)(128)(4,1)} %bitcast.225), calls=%async_computation.2 | async-start | bytes 3145728
  213.5 2.2 copy-start.2
  216.1 2.2 copy-start.5
